TPU v7x, 128 devices: a whole 4x4x4 slice. The times are simulated.
128 devices in a mesh: pool: 16 (over y, x), tensor: 8 (over z, core).
Axes of the slice: x: 4, y: 4, z: 4, core: 2. Of those that a mesh axis runs over, the one named last changes fastest.
Arguments:
- inputs: bfloat16 [1024, 8192], P(None, 'pool'), may hold values from -160 to 160
- attn_gain: bfloat16 [8192], P('pool'), may hold values from 0.5 to 1.5
- query_key_value_weight: bfloat16 [8192, 10240], P('pool', 'tensor'), may hold values from -0.0625 to 0.0625
- key_value_pages: bfloat16 [1024, 128, 8, 256], P('pool', None, 'tensor'), may hold values from -210 to 210, as said below
- w_out: bfloat16 [8192, 8192], P('tensor', 'pool'), may hold values from -0.5 to 0.5
- ffn_gain: bfloat16 [8192], P('pool'), may hold values from 0.5 to 1.5
- w_gate_up: bfloat16 [8192, 2, 28672], P('pool', None, 'tensor'), may hold values from -0.0625 to 0.0625
- w_down: bfloat16 [28672, 8192], P('tensor', 'pool'), may hold values from -0.0625 to 0.0625
- owner_pool_device: int32 [1024], replicated, may hold values from 0 to 15, as said below
- context_page_count: int32 [1024], replicated, may hold values from 1 to 8, as said below
- request_page_slots: int32 [1024, 8], replicated, may hold values from 0 to 63
- mig_page: int32 [16, 16], P('pool'), may hold values from 0 to 63
- mig_dest: int32 [16, 16], P('pool'), may hold values from 0 to 15, as said below
- mig_slot: int32 [16, 16], P('pool'), may hold values from 0 to 63, as said below
Outputs:
- out_rows: bfloat16 [1024, 8192], P(None, 'pool')
- new_pool: bfloat16 [1024, 128, 8, 256], P('pool', None, 'tensor')
Inputs may be any that keep to these rules, and one draw needn't show every extreme that they name: `key_value_pages`: cached keys (first 128 entries of the last dimension, rotary embedding already applied) and values (last 128). `owner_pool_device`: each aligned block of 64 requests names every pool device at most 8 times, and in every block one pool device is named exactly 8 times. `context_page_count`: at least one request has exactly 8 pages. `request_page_slots`: entries at or beyond a request's page count are not used. `mig_dest`: no row names one destination more than 2 times, and every row names one exactly 2 times. `mig_slot`: no two moved pages take the same slot of the same destination.
All inputs are finite; a program needn't handle non-finite values.
Results may differ from a plain program's by a relative error of at most 0.013.
Values may be sent and summed in bfloat16 or wider, within the bound.
No kernel may reach another device: no remote copies, remote signals or barrier semaphores. Data moves between devices by JAX's collectives and lax.ppermute only.
A program may use at most 192 MiB of HBM per device.

v0:
```python
import math
import jax
import jax.numpy as jnp
from jax import lax
from jax.sharding import PartitionSpec as P

MCAP = 2
epsilon = 1e-05


def rotate_halves(vectors, token_positions):
    half_dim = vectors.shape[-1] // 2
    steps_index = jnp.arange(half_dim, dtype=jnp.float32)
    frequency = jnp.exp(steps_index * (-2.0 * math.log(500000.0) / vectors.shape[-1]))
    angles = token_positions.astype(jnp.float32)[:, None] * frequency[None, :]
    cosine = jnp.cos(angles)[:, None, :]
    sine_part = jnp.sin(angles)[:, None, :]
    front_half = vectors[..., :half_dim]
    back_half = vectors[..., half_dim:]
    return jnp.concatenate(
        [front_half * cosine - back_half * sine_part, back_half * cosine + front_half * sine_part],
        axis=-1,
    )


def per_device(
    inputs,
    attn_gain,
    query_key_value_weight,
    key_value_pages,
    w_out,
    ffn_gain,
    w_gate_up,
    w_down,
    owner_pool_device,
    context_page_count,
    request_page_slots,
    mig_page,
    mig_dest,
    mig_slot,
):
    pool_count = lax.axis_size("pool")
    pool_here = lax.axis_index("pool")
    total_req = inputs.shape[0]
    per_block = total_req // pool_count
    local_width = inputs.shape[1]
    full_width = local_width * pool_count
    page_len = key_value_pages.shape[1]
    kv_local = key_value_pages.shape[2]
    head_dim = key_value_pages.shape[3] // 2
    query_groups = query_key_value_weight.shape[1] // (kv_local * head_dim) - 2
    capacity = max(2, (2 * per_block + pool_count - 1) // pool_count)
    scale = 1.0 / math.sqrt(head_dim)
    residual = inputs.astype(jnp.float32)
    squares = lax.psum(jnp.sum(residual * residual, axis=1), "pool")
    normed_input = (
        residual
        * lax.rsqrt(squares[:, None] / full_width + epsilon)
        * attn_gain.astype(jnp.float32)
    ).astype(jnp.bfloat16)
    block_owner = owner_pool_device.reshape(pool_count, per_block)
    pool_iota = jnp.arange(pool_count, dtype=jnp.int32)
    owner_hot = (block_owner[:, :, None] == pool_iota[None, None, :]).astype(jnp.int32)
    slot_rank = jnp.sum(jnp.cumsum(owner_hot, axis=1) * owner_hot, axis=2) - 1
    slot_iota = jnp.arange(capacity, dtype=jnp.int32)
    own_rows = lax.psum_scatter(
        jnp.dot(normed_input, query_key_value_weight, preferred_element_type=jnp.float32),
        "pool",
        scatter_dimension=0,
        tiled=True,
    )
    my_lengths = lax.dynamic_slice_in_dim(context_page_count, pool_here * per_block, per_block)
    token_positions = my_lengths * page_len
    item_count = own_rows.shape[0]
    parts = own_rows.reshape(item_count, kv_local, query_groups + 2, head_dim)
    query = rotate_halves(
        parts[:, :, :query_groups].reshape(item_count, kv_local * query_groups, head_dim),
        token_positions,
    ).reshape(item_count, kv_local, query_groups, head_dim)
    own_key = rotate_halves(parts[:, :, query_groups], token_positions)[:, :, None, :]
    own_val = parts[:, :, query_groups + 1][:, :, None, :]
    ready_rows = (
        jnp.concatenate([query, own_key, own_val], axis=2)
        .astype(jnp.bfloat16)
        .reshape(item_count, -1)
    )
    my_owner = block_owner[pool_here]
    my_rank = slot_rank[pool_here]
    slot_hits = (my_owner[:, None, None] == pool_iota[None, :, None]) & (
        my_rank[:, None, None] == slot_iota[None, None, :]
    )
    local_iota = jnp.arange(per_block, dtype=jnp.int32)
    local_pick = jnp.sum(jnp.where(slot_hits, local_iota[:, None, None], 0), axis=0)
    filled = jnp.any(slot_hits, axis=0)
    send_rows = jnp.where(
        filled[:, :, None], jnp.take(ready_rows, local_pick, axis=0), jnp.zeros((), jnp.bfloat16)
    )
    send_ids = jnp.where(filled, pool_here * per_block + local_pick, total_req)
    rows_all = lax.all_to_all(send_rows, "pool", split_axis=0, concat_axis=0, tiled=True)
    ids_all = lax.all_to_all(send_ids, "pool", split_axis=0, concat_axis=0, tiled=True)

    def one_block(blocks):
        rows_b, ids_b = blocks
        item_count = ids_b.shape[0]
        safe_ids = jnp.minimum(ids_b, total_req - 1)
        lengths = context_page_count[safe_ids]
        table = request_page_slots[safe_ids]
        context_span = table.shape[1] * page_len
        gathered_pages = key_value_pages[table].reshape(
            item_count, context_span, kv_local, 2 * head_dim
        )
        keys = gathered_pages[..., :head_dim]
        values = gathered_pages[..., head_dim:]
        parts = rows_b.reshape(item_count, kv_local, query_groups + 2, head_dim)
        query = parts[:, :, :query_groups]
        own_key = parts[:, :, query_groups]
        own_val = parts[:, :, query_groups + 1]
        scores = (
            jnp.einsum("nhgd,nthd->nhgt", query, keys, preferred_element_type=jnp.float32) * scale
        )
        valid = (jnp.arange(context_span)[None, :] < (lengths * page_len)[:, None])[
            :, None, None, :
        ]
        scores = jnp.where(valid, scores, -1e30)
        self_score = (
            jnp.einsum("nhgd,nhd->nhg", query, own_key, preferred_element_type=jnp.float32) * scale
        )
        top = jnp.maximum(jnp.max(scores, axis=-1), self_score)
        expo = jnp.where(valid, jnp.exp(scores - top[..., None]), 0.0)
        self_exp = jnp.exp(self_score - top)
        total = jnp.sum(expo, axis=-1) + self_exp
        weights = (expo / total[..., None]).astype(jnp.bfloat16)
        self_weight = (self_exp / total).astype(jnp.bfloat16)
        mixed = jnp.einsum("nhgt,nthd->nhgd", weights, values, preferred_element_type=jnp.float32)
        mixed = (
            mixed
            + self_weight.astype(jnp.float32)[..., None]
            * own_val.astype(jnp.float32)[:, :, None, :]
        )
        return mixed.astype(jnp.bfloat16).reshape(item_count, -1)

    attn_buf = lax.map(one_block, (rows_all, ids_all))
    returned = lax.all_to_all(attn_buf, "pool", split_axis=0, concat_axis=0, tiled=True)
    my_rows = returned[block_owner[pool_here], slot_rank[pool_here]]
    partial_value = jnp.dot(
        lax.all_gather(my_rows, "pool", axis=0, tiled=True),
        w_out,
        preferred_element_type=jnp.float32,
    )
    middle = residual + lax.psum(partial_value, "tensor")
    mid_squares = lax.psum(jnp.sum(middle * middle, axis=1), "pool")
    ffn_in = (
        middle
        * lax.rsqrt(mid_squares[:, None] / full_width + epsilon)
        * ffn_gain.astype(jnp.float32)
    ).astype(jnp.bfloat16)
    hidden_local = w_gate_up.shape[2]
    joined_weight = w_gate_up.reshape(local_width, 2 * hidden_local)
    gate_up = lax.psum_scatter(
        jnp.dot(ffn_in, joined_weight, preferred_element_type=jnp.float32),
        "pool",
        scatter_dimension=0,
        tiled=True,
    )
    hidden = (jax.nn.silu(gate_up[:, :hidden_local]) * gate_up[:, hidden_local:]).astype(
        jnp.bfloat16
    )
    down_part = jnp.dot(
        lax.all_gather(hidden, "pool", axis=0, tiled=True),
        w_down,
        preferred_element_type=jnp.float32,
    )
    out_rows = (
        middle + lax.psum(down_part.astype(jnp.bfloat16), "tensor").astype(jnp.float32)
    ).astype(jnp.bfloat16)
    move_pages = mig_page[0]
    move_dest = mig_dest[0]
    move_slot = mig_slot[0]
    move_count = move_pages.shape[0]
    local_slots = key_value_pages.shape[0]
    dest_hot = (move_dest[:, None] == pool_iota[None, :]).astype(jnp.int32)
    move_rank = jnp.sum(jnp.cumsum(dest_hot, axis=0) * dest_hot, axis=1) - 1
    cap_iota = jnp.arange(MCAP, dtype=jnp.int32)
    move_hits = (move_dest[:, None, None] == pool_iota[None, :, None]) & (
        move_rank[:, None, None] == cap_iota[None, None, :]
    )
    move_iota = jnp.arange(move_count, dtype=jnp.int32)
    move_pick = jnp.sum(jnp.where(move_hits, move_iota[:, None, None], 0), axis=0)
    move_filled = jnp.any(move_hits, axis=0)
    send_pages = jnp.where(
        move_filled[:, :, None, None, None],
        key_value_pages[move_pages[move_pick]],
        jnp.zeros((), jnp.bfloat16),
    )
    send_slots = jnp.where(move_filled, move_slot[move_pick], local_slots)
    got_pages, got_slots = (
        lax.all_to_all(send_pages, "pool", split_axis=0, concat_axis=0, tiled=True),
        lax.all_to_all(send_slots, "pool", split_axis=0, concat_axis=0, tiled=True),
    )
    new_pool = key_value_pages.at[got_slots.reshape(-1)].set(
        got_pages.reshape(-1, page_len, kv_local, 2 * head_dim), mode="drop"
    )
    return (out_rows, new_pool)


def solution(mesh):
    return jax.shard_map(
        per_device,
        mesh=mesh,
        in_specs=(
            P(None, "pool"),
            P("pool"),
            P("pool", "tensor"),
            P("pool", None, "tensor", None),
            P("tensor", "pool"),
            P("pool"),
            P("pool", None, "tensor"),
            P("tensor", "pool"),
            P(),
            P(),
            P(),
            P("pool", None),
            P("pool", None),
            P("pool", None),
        ),
        out_specs=(P(None, "pool"), P("pool", None, "tensor", None)),
        check_vma=False,
    )
```

profile of v0, /device:TPU:0, one launch (start us, length us, event | category | flops | bytes accessed | tf_op | source)
XLA Modules:
  0.0 855.2 jit_solution(3642810041750591851)
XLA Ops:
  12.4 40.7 %psum.28 = f32[1024]{0:T(1024)S(1)} all-reduce(f32[1024]{0:T(1024)S(1)} %fusion.20), channel_id=1, replica_groups=mesh['pool'=16,'tensor'=8] {'pool'}, use_global_device_ids=true, to_apply=%region_5.6 | all-reduce | flops 1024 | bytes 8192 | tf_op jit(solution)/shard_map/psum | solution.py:55
  64.9 68.5 %reduce-scatter.3.cloned.1.call-done = f32[64,1280]{1,0:T(8,128)} async-done(((f32[1024,1280]{1,0:T(8,128)}), f32[64,1280]{1,0:T(8,128)}) %reduce-scatter.3.cloned.1.call-update) | async-done | bytes 327696 | tf_op jit(solution)/shard_map/reduce_scatter | solution.py:66
  142.2 8.8 %all-to-all-done.1 = bf16[16,8,1280]{2,1,0:T(8,128)(2,1)S(1)} async-done(((bf16[16,8,1280]{2,1,0:T(8,128)(2,1)}), bf16[16,8,1280]{2,1,0:T(8,128)(2,1)S(1)}, u32[]{:S(2)}, u32[]{:S(2)}) %all-to-all-start.1) | async-done | bytes 327712 | tf_op jit(solution)/shard_map/all_to_all | solution.py:99
  151.0 187.4 %while.10 = (s32[]{:T(128)}, bf16[16,8,1024]{2,1,0:T(8,128)(2,1)}, s32[16,8]{1,0:T(8,128)S(1)}, s32[1024]{0:T(1024)S(1)}, bf16[16,8,1280]{2,1,0:T(8,128)(2,1)S(1...) while((s32[]{:T(128)}, bf16[16,8,1024]{2,1,0:T(8,128)(2,1)}, ...), condition=%wide.region_10.11_spmd, body=%wide.region_7.10_spmd.sunk | while | flops 34262696 | bytes 13621417 | solution.py:142
  152.6 4.9 gather_fusion.1
  164.3 4.9 gather_fusion.1
  176.0 4.9 gather_fusion.1
  187.7 4.9 gather_fusion.1
  199.4 4.9 gather_fusion.1
  211.1 4.9 gather_fusion.1
  222.8 4.9 gather_fusion.1
  234.5 4.9 gather_fusion.1
  246.2 4.9 gather_fusion.1
  258.0 4.9 gather_fusion.1
  269.7 4.9 gather_fusion.1
  281.4 4.9 gather_fusion.1
  293.1 4.9 gather_fusion.1
  304.8 4.9 gather_fusion.1
  328.2 4.9 gather_fusion.1
  342.0 8.6 %all-to-all-done.2 = bf16[16,8,1024]{2,1,0:T(8,128)(2,1)S(1)} async-done(((bf16[16,8,1024]{2,1,0:T(8,128)(2,1)}), bf16[16,8,1024]{2,1,0:T(8,128)(2,1)S(1)}, u32[]{:S(2)}, u32[]{:S(2)}) %all-to-all-start.2) | async-done | bytes 262176 | tf_op jit(solution)/shard_map/all_to_all | solution.py:143
  352.4 42.5 %all-gather.3.cloned.1.call-done = bf16[1024,1024]{1,0:T(8,128)(2,1)} async-done(((bf16[64,1024]{1,0:T(8,128)(2,1)}), bf16[1024,1024]{1,0:T(8,128)(2,1)}) %all-gather.3.cloned.1.call-update) | async-done | bytes 2097168 | tf_op jit(solution)/shard_map/all_gather | solution.py:146
  399.7 7.8 copy.104
  407.5 57.1 %all-reduce.3.cloned.1.call-done = f32[1024,512]{1,0:T(8,128)} async-done(((f32[1024,512]{1,0:T(8,128)}), f32[1024,512]{1,0:T(8,128)}) %all-reduce.3.cloned.1.call-update) | async-done | bytes 2097168 | tf_op jit(solution)/shard_map/psum | solution.py:150
  466.6 40.5 %psum.30 = f32[1024]{0:T(1024)S(1)} all-reduce(f32[1024]{0:T(1024)S(1)} %multiply_reduce_fusion), channel_id=1, replica_groups=mesh['pool'=16,'tensor'=8] {'pool'}, use_global_device_ids=true, to_apply=%region_13.14 | all-reduce | flops 1024 | bytes 8192 | tf_op jit(solution)/shard_map/psum | solution.py:151
  507.1 16.4 %fusion.23 = f32[1024,7168]{1,0:T(8,128)} fusion(bf16[512,7168]{1,0:T(8,128)(2,1)} %bitcast.147, f32[512]{0:T(512)S(1)} %convert_element_type.70, f32[1024]{0:T(1024)S(1)} %add_rsqrt_fusion, f32[1024,512]{1,0:T(8,128)} %all-reduce.3.cloned.1.call-done, bf16[1024,512]{1,0:T(8,128)(2,1)S(1)} %copy-done.5), kind=kOutput, calls=%fused_computation.59 | convolution fusion | flops 7518814208 | bytes 39852032 | tf_op jit(solution)/shard_map/dot_general | solution.py:160
  523.6 168.2 %reduce-scatter.5.cloned.1.call-done = f32[64,7168]{1,0:T(8,128)} async-done(((f32[1024,7168]{1,0:T(8,128)}), f32[64,7168]{1,0:T(8,128)}) %reduce-scatter.5.cloned.1.call-update) | async-done | bytes 1835024 | tf_op jit(solution)/shard_map/reduce_scatter | solution.py:159
  696.5 5.3 all-to-all-start.3
  710.6 7.3 all-to-all-start.4
  718.0 55.6 %all-gather.5.cloned.1.call-done = bf16[1024,3584]{1,0:T(8,128)(2,1)} async-done(((bf16[64,3584]{1,0:T(8,128)(2,1)}), bf16[1024,3584]{1,0:T(8,128)(2,1)}) %all-gather.5.cloned.1.call-update) | async-done | bytes 7340048 | tf_op jit(solution)/shard_map/all_gather | solution.py:169
  773.6 9.0 %convolution_convert_fusion = bf16[1024,512]{1,0:T(8,128)(2,1)} fusion(bf16[1024,3584]{1,0:T(8,128)(2,1)} %all-gather.5.cloned.1.call-done, bf16[3584,512]{1,0:T(8,128)(2,1)} %param.23), kind=kOutput, calls=%fused_computation.58 | convolution fusion | flops 3758620672 | bytes 12058624 | tf_op jit(solution)/shard_map/dot_general | solution.py:168
  784.1 6.0 scatter_fusion
  790.1 55.0 %all-reduce.5.cloned.1.call-done = bf16[1024,512]{1,0:T(8,128)(2,1)} async-done(((bf16[1024,512]{1,0:T(8,128)(2,1)}), bf16[1024,512]{1,0:T(8,128)(2,1)}) %all-reduce.5.cloned.1.call-update) | async-done | bytes 1048592 | tf_op jit(solution)/shard_map/psum | solution.py:174
  (440 shorter events, 168.7 us)
Async XLA Ops:
  7.2 46.0 %copy-start = (bf16[512,1280]{1,0:T(8,128)(2,1)S(1)}, bf16[512,1280]{1,0:T(8,128)(2,1)}, u32[]{:S(2)}) copy-start(bf16[512,1280]{1,0:T(8,128)(2,1)} %param.18) | copy-start | bytes 3932164
  7.2 4.9 copy-start.5
  7.2 4.9 copy-start.9
  7.2 126.2 %reduce-scatter.3.cloned.1.call-start = ((), (), s32[]{:S(2)}) async-start(), calls=%async_computation.7 | async-start | bytes 5570560 | tf_op jit(solution)/shard_map/reduce_scatter | solution.py:66
  57.0 0.7 copy-start.7
  57.0 7.6 copy-start.4
  60.9 76.2 %all-to-all-start = ((s32[16,1,8]{2,1,0:T(1,128)}), s32[16,1,8]{2,1,0:T(1,128)S(1)}, u32[]{:S(2)}, u32[]{:S(2)}) async-start(s32[16,1,8]{2,1,0:T(1,128)} %bitcast.37), calls=%async_computation | async-start | bytes 16384 | tf_op jit(solution)/shard_map/all_to_all | solution.py:100
  135.3 6.6 copy-start.6
  137.1 13.9 %all-to-all-start.1 = ((bf16[16,8,1280]{2,1,0:T(8,128)(2,1)}), bf16[16,8,1280]{2,1,0:T(8,128)(2,1)S(1)}, u32[]{:S(2)}, u32[]{:S(2)}) async-start(bf16[16,8,1280]{2,1,0:T(8,128)(2,1)} %fusion.33), calls=%async_computation.2 | async-start | bytes 655360 | tf_op jit(solution)/shard_map/all_to_all | solution.py:99
  151.0 243.8 %copy-start.11 = (bf16[1024,512]{1,0:T(8,128)(2,1)S(1)}, bf16[1024,512]{1,0:T(8,128)(2,1)}, u32[]{:S(2)}) copy-start(bf16[1024,512]{1,0:T(8,128)(2,1)} %param.20) | copy-start | bytes 3145732
  338.4 12.2 %all-to-all-start.2 = ((bf16[16,8,1024]{2,1,0:T(8,128)(2,1)}), bf16[16,8,1024]{2,1,0:T(8,128)(2,1)S(1)}, u32[]{:S(2)}, u32[]{:S(2)}) async-start(bf16[16,8,1024]{2,1,0:T(8,128)(2,1)} %get-tuple-element.39), calls=%async_computation.3 | async-start | bytes 524288 | tf_op jit(solution)/shard_map/all_to_all | solution.py:143
  341.9 52.9 %all-gather.3.cloned.1.call-start = ((), (), s32[]{:S(2)}) async-start(), calls=%async_computation.8 | async-start | bytes 2228224 | tf_op jit(solution)/shard_map/all_gather | solution.py:146
  352.3 112.3 %all-reduce.3.cloned.1.call-start = ((), (), s32[]{:S(2)}) async-start(), calls=%async_computation.9 | async-start | bytes 4194304 | tf_op jit(solution)/shard_map/psum | solution.py:150
  399.0 0.7 copy-start.10
  399.0 292.7 %reduce-scatter.5.cloned.1.call-start = ((), (), s32[]{:S(2)}) async-start(), calls=%async_computation.10 | async-start | bytes 31195136 | tf_op jit(solution)/shard_map/reduce_scatter | solution.py:159
  523.5 170.7 %copy-start.8 = (s32[1,16]{1,0:T(1,128)S(1)}, s32[1,16]{1,0:T(1,128)}, u32[]{:S(2)}) copy-start(s32[1,16]{1,0:T(1,128)} %param.28) | copy-start | bytes 196
  523.5 171.3 %copy-start.2 = (s32[1,16]{1,0:T(1,128)S(1)}, s32[1,16]{1,0:T(1,128)}, u32[]{:S(2)}) copy-start(s32[1,16]{1,0:T(1,128)} %param.29) | copy-start | bytes 196
  523.5 250.1 %all-gather.5.cloned.1.call-start = ((), (), s32[]{:S(2)}) async-start(), calls=%async_computation.11 | async-start | bytes 7798784 | tf_op jit(solution)/shard_map/all_gather | solution.py:169
  695.6 6.4 copy-start.3
  696.5 14.1 %all-to-all-start.3 = ((s32[16,1,2]{2,1,0:T(1,128)}), s32[16,1,2]{2,1,0:T(1,128)S(1)}, u32[]{:S(2)}, u32[]{:S(2)}) async-start(s32[16,1,2]{2,1,0:T(1,128)} %copy.91), calls=%async_computation.5 | async-start | bytes 16384 | tf_op jit(solution)/shard_map/all_to_all | solution.py:198
  710.6 73.5 %all-to-all-start.4 = ((bf16[16,2,128,1,256]{4,2,1,3,0:T(8,128)(2,1)}), bf16[16,2,128,1,256]{4,2,1,3,0:T(8,128)(2,1)}, u32[]{:S(2)}, u32[]{:S(2)}) async-start(bf16[16,2,128,1,256]{4,2,1,3,0:T(8,128)(2,1)} %broadcast_select_fusion), calls=%async_computation.6 | async-start | bytes 4194304 | tf_op jit(solution)/shard_map/all_to_all | solution.py:197
  718.0 127.1 %all-reduce.5.cloned.1.call-start = ((), (), s32[]{:S(2)}) async-start(), calls=%async_computation.12 | async-start | bytes 2097152 | tf_op jit(solution)/shard_map/psum | solution.py:174
  784.1 64.3 %copy-start.1 = (bf16[512,1280]{1,0:T(8,128)(2,1)S(1)}, bf16[512,1280]{1,0:T(8,128)(2,1)}, u32[]{:S(2)}) copy-start(bf16[512,1280]{1,0:T(8,128)(2,1)} %param.18) | copy-start | bytes 3932164
Sparse Core Ops, SparseCore 0:
  57.2 76.1 reduce-scatter.2
  352.4 42.3 all-gather.2
  399.2 65.4 all-reduce.2
  523.6 168.0 reduce-scatter.4
  694.4 79.2 all-gather.4
  782.8 62.1 all-reduce.4
where the time goes:
time: 858 us; the launch traced here: 855 us
  waiting for transfers between devices  464 us (54%)
  local copies, waits for them, and re-layouts  142 us (17%)
  matrix products  105 us (12%)
  blocking collectives  81.2 us (9%)
  starting transfers between devices  24.8 us (3%)
  other arithmetic  22.7 us (3%)
  between operations  14.5 us (2%)
    reduce_scatter x1, waiting for transfers between devices, per_device(): lax.psum_scatter(jnp.dot(ffn_in, joined_weight, preferred_element_type=jn...  168 us
    gather x16, local copies, waits for them, and re-layouts, one_block(): key_value_pages[table]  78.9 us
    reduce_scatter x1, waiting for transfers between devices, per_device(): lax.psum_scatter(jnp.dot(normed_input, query_key_value_weight, preferred_...  68.5 us
    psum x1, waiting for transfers between devices, per_device(): middle = residual + lax.psum(partial_value, 'tensor')  57.1 us
    all_gather x1, waiting for transfers between devices, per_device(): lax.all_gather(hidden, 'pool', axis=0, tiled=True)  55.6 us
    psum x1, waiting for transfers between devices, per_device(): lax.psum(down_part.astype(jnp.bfloat16), 'tensor').astype(jnp.float32)  55 us
    all_gather x1, waiting for transfers between devices, per_device(): lax.all_gather(my_rows, 'pool', axis=0, tiled=True)  42.5 us
    psum x1, blocking collectives, per_device(): squares = lax.psum(jnp.sum(residual * residual, axis=1), 'pool')  40.7 us
  transfers between devices with their start and end apart: 11, of which 8 were waited for; matrix products, arithmetic and copies ran while one was open for 5% of the time, Pallas kernels for 0%

commit v1 on v0

--- a/solution.py
+++ b/solution.py
@@ -165,11 +165,36 @@
     hidden = (jax.nn.silu(gate_up[:, :hidden_local]) * gate_up[:, hidden_local:]).astype(
         jnp.bfloat16
     )
-    down_part = jnp.dot(
-        lax.all_gather(hidden, "pool", axis=0, tiled=True),
-        w_down,
-        preferred_element_type=jnp.float32,
-    )
+
+    def _draw_loops(field_in):
+        y2, work_now, local_out = (lax.axis_size("pool"), lax.axis_index("pool"), field_in.shape[0])
+        block_now = v1 = field_in
+        tile_out = lax.dynamic_update_slice_in_dim(
+            jnp.zeros(
+                [num * y2 if j == 0 else num for j, num in enumerate(field_in.shape)],
+                field_in.dtype,
+            ),
+            field_in,
+            work_now * local_out,
+            axis=0,
+        )
+        for p in range(1, y2 // 2 + 1):
+            block_now = lax.ppermute(
+                block_now, "pool", perm=list(map(lambda j: (j, (j + 1) % y2), range(y2)))
+            )
+            tile_out = lax.dynamic_update_slice_in_dim(
+                tile_out, block_now, (work_now - p) % y2 * local_out, axis=0
+            )
+            if 2 * p < y2:
+                v1 = lax.ppermute(
+                    v1, "pool", perm=list(map(lambda j: (j, (j - 1) % y2), range(y2)))
+                )
+                tile_out = lax.dynamic_update_slice_in_dim(
+                    tile_out, v1, (work_now + p) % y2 * local_out, axis=0
+                )
+        return tile_out
+
+    down_part = jnp.dot(_draw_loops(hidden), w_down, preferred_element_type=jnp.float32)
     out_rows = (
         middle + lax.psum(down_part.astype(jnp.bfloat16), "tensor").astype(jnp.float32)
     ).astype(jnp.bfloat16)

time: 858 us -> 899 us (1.048)
  starting transfers between devices: 24.8 us -> 60.1 us
  local copies, waits for them, and re-layouts: 142 us -> 157 us
    ppermute x0 -> x15, waiting for transfers between devices: none -> 57.2 us  [the longest x8 57.2 us: _draw_loops(): lax.ppermute(block_now, 'pool', perm=list(map(lambda j: (j, (j + 1) % y2)...]
    all_gather x1 -> x0, waiting for transfers between devices: 55.6 us -> none  [per_device(): lax.all_gather(hidden, 'pool', axis=0, tiled=True)]
    ppermute x0 -> x15, starting transfers between devices: none -> 37.5 us  [the longest x7 36.2 us: _draw_loops(): lax.ppermute(v1, 'pool', perm=list(map(lambda j: (j, (j - 1) % y2), range...]
    dynamic_update_slice x0 -> x15, local copies, waits for them, and re-layouts: none -> 12.2 us  [the longest x8 6.52 us: _draw_loops(): lax.dynamic_update_slice_in_dim(tile_out, block_now, (work_now - p) % y2...]
  transfers between devices with their start and end apart: 11 -> 25, of which waited for: 8 -> 15; matrix products, arithmetic and copies ran while one was open for 5% -> 7% of each run, Pallas kernels for 0% -> 0%
where the time goes in v1:
time: 899 us; the launch traced here: 896 us
  waiting for transfers between devices  456 us (51%)
  local copies, waits for them, and re-layouts  157 us (17%)
  matrix products  105 us (12%)
  blocking collectives  81.2 us (9%)
  starting transfers between devices  60.1 us (7%)
  other arithmetic  21.2 us (2%)
  between operations  14.3 us (2%)
    reduce_scatter x1, waiting for transfers between devices, per_device(): lax.psum_scatter(jnp.dot(ffn_in, joined_weight, preferred_element_type=jn...  161 us
    gather x16, local copies, waits for them, and re-layouts, one_block(): key_value_pages[table]  79.1 us
    reduce_scatter x1, waiting for transfers between devices, per_device(): lax.psum_scatter(jnp.dot(normed_input, query_key_value_weight, preferred_...  68.6 us
    psum x1, waiting for transfers between devices, per_device(): middle = residual + lax.psum(partial_value, 'tensor')  57.7 us
    ppermute x8, waiting for transfers between devices, _draw_loops(): lax.ppermute(block_now, 'pool', perm=list(map(lambda j: (j, (j + 1) % y2)...  57.2 us
    psum x1, waiting for transfers between devices, per_device(): lax.psum(down_part.astype(jnp.bfloat16), 'tensor').astype(jnp.float32)  52.1 us
    all_gather x1, waiting for transfers between devices, per_device(): lax.all_gather(my_rows, 'pool', axis=0, tiled=True)  42.5 us
    psum x1, blocking collectives, per_device(): squares = lax.psum(jnp.sum(residual * residual, axis=1), 'pool')  40.7 us
  transfers between devices with their start and end apart: 25, of which 15 were waited for; matrix products, arithmetic and copies ran while one was open for 7% of the time, Pallas kernels for 0%

profile of v1, /device:TPU:0, one launch (start us, length us, event | category | flops | bytes accessed | tf_op | source)
XLA Modules:
  0.0 896.5 jit_solution(8981586879267934674)
XLA Ops:
  12.4 40.7 %psum.28 = f32[1024]{0:T(1024)S(1)} all-reduce(f32[1024]{0:T(1024)S(1)} %fusion.20), channel_id=1, replica_groups=mesh['pool'=16,'tensor'=8] {'pool'}, use_global_device_ids=true, to_apply=%region_5.6 | all-reduce | flops 1024 | bytes 8192 | tf_op jit(solution)/shard_map/psum | solution.py:55
  64.9 68.6 %reduce-scatter.3.cloned.1.call-done = f32[64,1280]{1,0:T(8,128)} async-done(((f32[1024,1280]{1,0:T(8,128)}), f32[64,1280]{1,0:T(8,128)}) %reduce-scatter.3.cloned.1.call-update) | async-done | bytes 327696 | tf_op jit(solution)/shard_map/reduce_scatter | solution.py:66
  142.2 8.8 all-to-all-done.1
  151.0 187.6 %while.10 = (s32[]{:T(128)}, bf16[16,8,1024]{2,1,0:T(8,128)(2,1)}, s32[16,8]{1,0:T(8,128)S(1)}, s32[1024]{0:T(1024)S(1)}, bf16[16,8,1280]{2,1,0:T(8,128)(2,1)S(1...) while((s32[]{:T(128)}, bf16[16,8,1024]{2,1,0:T(8,128)(2,1)}, ...), condition=%wide.region_10.11_spmd, body=%wide.region_7.10_spmd.sunk | while | flops 34262696 | bytes 13621917 | solution.py:142
  163.4 4.9 gather_fusion.1
  175.2 4.9 gather_fusion.1
  222.1 4.9 gather_fusion.1
  269.0 4.9 gather_fusion.1
  292.4 4.9 gather_fusion.1
  342.3 8.6 all-to-all-done.2
  352.7 42.5 %all-gather.2.cloned.1.call-done = bf16[1024,1024]{1,0:T(8,128)(2,1)} async-done(((bf16[64,1024]{1,0:T(8,128)(2,1)}), bf16[1024,1024]{1,0:T(8,128)(2,1)}) %all-gather.2.cloned.1.call-update) | async-done | bytes 2097168 | tf_op jit(solution)/shard_map/all_gather | solution.py:146
  399.4 7.8 copy.104
  407.2 57.7 %all-reduce.3.cloned.1.call-done = f32[1024,512]{1,0:T(8,128)} async-done(((f32[1024,512]{1,0:T(8,128)}), f32[1024,512]{1,0:T(8,128)}) %all-reduce.3.cloned.1.call-update) | async-done | bytes 2097168 | tf_op jit(solution)/shard_map/psum | solution.py:150
  466.8 40.5 %psum.30 = f32[1024]{0:T(1024)S(1)} all-reduce(f32[1024]{0:T(1024)S(1)} %multiply_reduce_fusion), channel_id=1, replica_groups=mesh['pool'=16,'tensor'=8] {'pool'}, use_global_device_ids=true, to_apply=%region_13.14 | all-reduce | flops 1024 | bytes 8192 | tf_op jit(solution)/shard_map/psum | solution.py:151
  507.3 16.4 %fusion.23 = f32[1024,7168]{1,0:T(8,128)} fusion(bf16[512,7168]{1,0:T(8,128)(2,1)} %bitcast.146, f32[512]{0:T(512)S(1)} %convert_element_type.70, f32[1024]{0:T(1024)S(1)} %add_rsqrt_fusion, f32[1024,512]{1,0:T(8,128)} %all-reduce.3.cloned.1.call-done, bf16[1024,512]{1,0:T(8,128)(2,1)S(1)} %copy-done.5), kind=kOutput, calls=%fused_computation.59 | convolution fusion | flops 7518814208 | bytes 39852032 | tf_op jit(solution)/shard_map/dot_general | solution.py:160
  531.1 161.0 %reduce-scatter.5.cloned.1.call-done = f32[64,7168]{1,0:T(8,128)} async-done(((f32[1024,7168]{1,0:T(8,128)}), f32[64,7168]{1,0:T(8,128)}) %reduce-scatter.5.cloned.1.call-update) | async-done | bytes 1835024 | tf_op jit(solution)/shard_map/reduce_scatter | solution.py:159
  712.2 5.3 collective-permute-start.3
  719.2 7.8 collective-permute-done.2
  727.0 5.3 collective-permute-start.5
  733.9 6.9 collective-permute-done.4
  740.8 5.3 collective-permute-start.7
  747.8 6.0 collective-permute-done.6
  753.7 5.3 collective-permute-start.9
  760.8 5.0 collective-permute-done.8
  765.7 5.3 collective-permute-start.11
  777.5 5.5 collective-permute-start.13
  784.6 5.7 collective-permute-done.12
  791.9 6.8 all-to-all-start.4
  799.0 18.5 %collective-permute-done.14 = bf16[64,3584]{1,0:T(8,128)(2,1)S(1)} collective-permute-done((bf16[64,3584]{1,0:T(8,128)(2,1)S(1)}, bf16[64,3584]{1,0:T(8,128)(2,1)S(1)}, u32[]{:S(2)}, u32[]{:S(2)}) %collective-permute-start.14) | collective-permute-done | bytes 458784 | tf_op jit(solution)/shard_map/ppermute | solution.py:182
  818.3 9.0 %convolution_convert_fusion = bf16[1024,512]{1,0:T(8,128)(2,1)} fusion(bf16[1024,3584]{1,0:T(8,128)(2,1)} %constant_dynamic-update-slice_fusion.1, bf16[3584,512]{1,0:T(8,128)(2,1)} %param.23), kind=kOutput, calls=%fused_computation.58 | convolution fusion | flops 3758620672 | bytes 12058624 | tf_op jit(solution)/shard_map/dot_general | solution.py:197
  828.6 6.0 scatter_fusion
  834.6 52.1 %all-reduce.5.cloned.1.call-done = bf16[1024,512]{1,0:T(8,128)(2,1)} async-done(((bf16[1024,512]{1,0:T(8,128)(2,1)}), bf16[1024,512]{1,0:T(8,128)(2,1)}) %all-reduce.5.cloned.1.call-update) | async-done | bytes 1048592 | tf_op jit(solution)/shard_map/psum | solution.py:199
  (485 shorter events, 248.3 us)
Async XLA Ops:
  7.2 46.0 %copy-start = (bf16[512,1280]{1,0:T(8,128)(2,1)S(1)}, bf16[512,1280]{1,0:T(8,128)(2,1)}, u32[]{:S(2)}) copy-start(bf16[512,1280]{1,0:T(8,128)(2,1)} %param.18) | copy-start | bytes 3932164
  7.2 45.9 %copy-start.10 = (bf16[512]{0:T(512)(128)(2,1)S(1)}, bf16[512]{0:T(512)(128)(2,1)}, u32[]{:S(2)}) copy-start(bf16[512]{0:T(512)(128)(2,1)} %param.17) | copy-start | bytes 3076
  7.2 126.3 %reduce-scatter.3.cloned.1.call-start = ((), (), s32[]{:S(2)}) async-start(), calls=%async_computation.7 | async-start | bytes 5570560 | tf_op jit(solution)/shard_map/reduce_scatter | solution.py:66
  57.1 7.5 copy-start.4
  59.3 82.7 %copy-start.7 = (s32[1024,8]{0,1:T(8,128)S(1)}, s32[1024,8]{0,1:T(8,128)}, u32[]{:S(2)}) copy-start(s32[1024,8]{0,1:T(8,128)} %param.26) | copy-start | bytes 98308
  60.9 76.2 %all-to-all-start = ((s32[16,1,8]{2,1,0:T(1,128)}), s32[16,1,8]{2,1,0:T(1,128)S(1)}, u32[]{:S(2)}, u32[]{:S(2)}) async-start(s32[16,1,8]{2,1,0:T(1,128)} %bitcast.37), calls=%async_computation | async-start | bytes 16384 | tf_op jit(solution)/shard_map/all_to_all | solution.py:100
  137.1 13.9 %all-to-all-start.1 = ((bf16[16,8,1280]{2,1,0:T(8,128)(2,1)}), bf16[16,8,1280]{2,1,0:T(8,128)(2,1)S(1)}, u32[]{:S(2)}, u32[]{:S(2)}) async-start(bf16[16,8,1280]{2,1,0:T(8,128)(2,1)} %fusion.33), calls=%async_computation.2 | async-start | bytes 655360 | tf_op jit(solution)/shard_map/all_to_all | solution.py:99
  151.0 244.1 %copy-start.12 = (bf16[1024,512]{1,0:T(8,128)(2,1)S(1)}, bf16[1024,512]{1,0:T(8,128)(2,1)}, u32[]{:S(2)}) copy-start(bf16[1024,512]{1,0:T(8,128)(2,1)} %param.20) | copy-start | bytes 3145732
  338.7 12.2 %all-to-all-start.2 = ((bf16[16,8,1024]{2,1,0:T(8,128)(2,1)}), bf16[16,8,1024]{2,1,0:T(8,128)(2,1)S(1)}, u32[]{:S(2)}, u32[]{:S(2)}) async-start(bf16[16,8,1024]{2,1,0:T(8,128)(2,1)} %get-tuple-element.39), calls=%async_computation.3 | async-start | bytes 524288 | tf_op jit(solution)/shard_map/all_to_all | solution.py:143
  342.2 52.9 %all-gather.2.cloned.1.call-start = ((), (), s32[]{:S(2)}) async-start(), calls=%async_computation.8 | async-start | bytes 2228224 | tf_op jit(solution)/shard_map/all_gather | solution.py:146
  352.6 112.3 %all-reduce.3.cloned.1.call-start = ((), (), s32[]{:S(2)}) async-start(), calls=%async_computation.9 | async-start | bytes 4194304 | tf_op jit(solution)/shard_map/psum | solution.py:150
  399.3 292.8 %reduce-scatter.5.cloned.1.call-start = ((), (), s32[]{:S(2)}) async-start(), calls=%async_computation.10 | async-start | bytes 31195136 | tf_op jit(solution)/shard_map/reduce_scatter | solution.py:159
  399.4 7.8 copy-start.11
  526.7 265.2 %all-to-all-start.3 = ((s32[16,1,2]{2,1,0:T(1,128)}), s32[16,1,2]{2,1,0:T(1,128)S(1)}, u32[]{:S(2)}, u32[]{:S(2)}) async-start(s32[16,1,2]{2,1,0:T(1,128)} %copy.91), calls=%async_computation.5 | async-start | bytes 16384 | tf_op jit(solution)/shard_map/all_to_all | solution.py:223
  696.6 15.6 %collective-permute-start = (bf16[64,3584]{1,0:T(8,128)(2,1)S(1)}, bf16[64,3584]{1,0:T(8,128)(2,1)S(1)}, u32[]{:S(2)}, u32[]{:S(2)}) collective-permute-start(bf16[64,3584]{1,0:T(8,128)(2,1)S(1)} %get-tuple-element.90), channel_id=1, source_target_pairs={{0,8},{8,16},{16,24},{24,32},{32,40},{40,48},{48,56},{56,64},{64,7... | collective-permute-start | bytes 1376264 | tf_op jit(solution)/shard_map/ppermute | solution.py:182
  697.9 14.3 %collective-permute-start.1 = (bf16[64,3584]{1,0:T(8,128)(2,1)S(1)}, bf16[64,3584]{1,0:T(8,128)(2,1)S(1)}, u32[]{:S(2)}, u32[]{:S(2)}) collective-permute-start(bf16[64,3584]{1,0:T(8,128)(2,1)S(1)} %get-tuple-element.90), channel_id=1, source_target_pairs={{0,120},{8,0},{16,8},{24,16},{32,24},{40,32},{48,40},{56,48},{64,5... | collective-permute-start | bytes 1376264 | tf_op jit(solution)/shard_map/ppermute | solution.py:189
  712.2 14.8 %collective-permute-start.2 = (bf16[64,3584]{1,0:T(8,128)(2,1)S(1)}, bf16[64,3584]{1,0:T(8,128)(2,1)S(1)}, u32[]{:S(2)}, u32[]{:S(2)}) collective-permute-start(bf16[64,3584]{1,0:T(8,128)(2,1)S(1)} %collective-permute-done), channel_id=1, source_target_pairs={{0,8},{8,16},{16,24},{24,32},{32,40},{40,48},{48,56},{56,64},{64,7... | collective-permute-start | bytes 1376264 | tf_op jit(solution)/shard_map/ppermute | solution.py:182
  712.2 14.8 %collective-permute-start.3 = (bf16[64,3584]{1,0:T(8,128)(2,1)S(1)}, bf16[64,3584]{1,0:T(8,128)(2,1)S(1)}, u32[]{:S(2)}, u32[]{:S(2)}) collective-permute-start(bf16[64,3584]{1,0:T(8,128)(2,1)S(1)} %collective-permute-done.1), channel_id=1, source_target_pairs={{0,120},{8,0},{16,8},{24,16},{32,24},{40,32},{48,40},{56,48},{64,5... | collective-permute-start | bytes 1376264 | tf_op jit(solution)/shard_map/ppermute | solution.py:189
  727.0 13.8 %collective-permute-start.4 = (bf16[64,3584]{1,0:T(8,128)(2,1)S(1)}, bf16[64,3584]{1,0:T(8,128)(2,1)S(1)}, u32[]{:S(2)}, u32[]{:S(2)}) collective-permute-start(bf16[64,3584]{1,0:T(8,128)(2,1)S(1)} %collective-permute-done.2), channel_id=1, source_target_pairs={{0,8},{8,16},{16,24},{24,32},{32,40},{40,48},{48,56},{56,64},{64,7... | collective-permute-start | bytes 1376264 | tf_op jit(solution)/shard_map/ppermute | solution.py:182
  727.0 13.8 %collective-permute-start.5 = (bf16[64,3584]{1,0:T(8,128)(2,1)S(1)}, bf16[64,3584]{1,0:T(8,128)(2,1)S(1)}, u32[]{:S(2)}, u32[]{:S(2)}) collective-permute-start(bf16[64,3584]{1,0:T(8,128)(2,1)S(1)} %collective-permute-done.3), channel_id=1, source_target_pairs={{0,120},{8,0},{16,8},{24,16},{32,24},{40,32},{48,40},{56,48},{64,5... | collective-permute-start | bytes 1376264 | tf_op jit(solution)/shard_map/ppermute | solution.py:189
  740.8 12.9 %collective-permute-start.6 = (bf16[64,3584]{1,0:T(8,128)(2,1)S(1)}, bf16[64,3584]{1,0:T(8,128)(2,1)S(1)}, u32[]{:S(2)}, u32[]{:S(2)}) collective-permute-start(bf16[64,3584]{1,0:T(8,128)(2,1)S(1)} %collective-permute-done.4), channel_id=1, source_target_pairs={{0,8},{8,16},{16,24},{24,32},{32,40},{40,48},{48,56},{56,64},{64,7... | collective-permute-start | bytes 1376264 | tf_op jit(solution)/shard_map/ppermute | solution.py:182
  740.8 12.9 %collective-permute-start.7 = (bf16[64,3584]{1,0:T(8,128)(2,1)S(1)}, bf16[64,3584]{1,0:T(8,128)(2,1)S(1)}, u32[]{:S(2)}, u32[]{:S(2)}) collective-permute-start(bf16[64,3584]{1,0:T(8,128)(2,1)S(1)} %collective-permute-done.5), channel_id=1, source_target_pairs={{0,120},{8,0},{16,8},{24,16},{32,24},{40,32},{48,40},{56,48},{64,5... | collective-permute-start | bytes 1376264 | tf_op jit(solution)/shard_map/ppermute | solution.py:189
  753.7 12.0 %collective-permute-start.8 = (bf16[64,3584]{1,0:T(8,128)(2,1)S(1)}, bf16[64,3584]{1,0:T(8,128)(2,1)S(1)}, u32[]{:S(2)}, u32[]{:S(2)}) collective-permute-start(bf16[64,3584]{1,0:T(8,128)(2,1)S(1)} %collective-permute-done.6), channel_id=1, source_target_pairs={{0,8},{8,16},{16,24},{24,32},{32,40},{40,48},{48,56},{56,64},{64,7... | collective-permute-start | bytes 1376264 | tf_op jit(solution)/shard_map/ppermute | solution.py:182
  753.7 12.0 %collective-permute-start.9 = (bf16[64,3584]{1,0:T(8,128)(2,1)S(1)}, bf16[64,3584]{1,0:T(8,128)(2,1)S(1)}, u32[]{:S(2)}, u32[]{:S(2)}) collective-permute-start(bf16[64,3584]{1,0:T(8,128)(2,1)S(1)} %collective-permute-done.7), channel_id=1, source_target_pairs={{0,120},{8,0},{16,8},{24,16},{32,24},{40,32},{48,40},{56,48},{64,5... | collective-permute-start | bytes 1376264 | tf_op jit(solution)/shard_map/ppermute | solution.py:189
  765.7 11.8 %collective-permute-start.10 = (bf16[64,3584]{1,0:T(8,128)(2,1)S(1)}, bf16[64,3584]{1,0:T(8,128)(2,1)S(1)}, u32[]{:S(2)}, u32[]{:S(2)}) collective-permute-start(bf16[64,3584]{1,0:T(8,128)(2,1)S(1)} %collective-permute-done.8), channel_id=1, source_target_pairs={{0,8},{8,16},{16,24},{24,32},{32,40},{40,48},{48,56},{56,64},{64,7... | collective-permute-start | bytes 1376264 | tf_op jit(solution)/shard_map/ppermute | solution.py:182
  765.7 11.8 %collective-permute-start.11 = (bf16[64,3584]{1,0:T(8,128)(2,1)S(1)}, bf16[64,3584]{1,0:T(8,128)(2,1)S(1)}, u32[]{:S(2)}, u32[]{:S(2)}) collective-permute-start(bf16[64,3584]{1,0:T(8,128)(2,1)S(1)} %collective-permute-done.9), channel_id=1, source_target_pairs={{0,120},{8,0},{16,8},{24,16},{32,24},{40,32},{48,40},{56,48},{64,5... | collective-permute-start | bytes 1376264 | tf_op jit(solution)/shard_map/ppermute | solution.py:189
  777.5 12.8 %collective-permute-start.12 = (bf16[64,3584]{1,0:T(8,128)(2,1)S(1)}, bf16[64,3584]{1,0:T(8,128)(2,1)S(1)}, u32[]{:S(2)}, u32[]{:S(2)}) collective-permute-start(bf16[64,3584]{1,0:T(8,128)(2,1)S(1)} %collective-permute-done.10), channel_id=1, source_target_pairs={{0,8},{8,16},{16,24},{24,32},{32,40},{40,48},{48,56},{56,64},{64,7... | collective-permute-start | bytes 1376264 | tf_op jit(solution)/shard_map/ppermute | solution.py:182
  777.5 13.6 %collective-permute-start.13 = (bf16[64,3584]{1,0:T(8,128)(2,1)S(1)}, bf16[64,3584]{1,0:T(8,128)(2,1)S(1)}, u32[]{:S(2)}, u32[]{:S(2)}) collective-permute-start(bf16[64,3584]{1,0:T(8,128)(2,1)S(1)} %collective-permute-done.11), channel_id=1, source_target_pairs={{0,120},{8,0},{16,8},{24,16},{32,24},{40,32},{48,40},{56,48},{64,5... | collective-permute-start | bytes 1376264 | tf_op jit(solution)/shard_map/ppermute | solution.py:189
  790.3 27.2 %collective-permute-start.14 = (bf16[64,3584]{1,0:T(8,128)(2,1)S(1)}, bf16[64,3584]{1,0:T(8,128)(2,1)S(1)}, u32[]{:S(2)}, u32[]{:S(2)}) collective-permute-start(bf16[64,3584]{1,0:T(8,128)(2,1)S(1)} %collective-permute-done.12), channel_id=1, source_target_pairs={{0,8},{8,16},{16,24},{24,32},{32,40},{40,48},{48,56},{56,64},{64,7... | collective-permute-start | bytes 1376264 | tf_op jit(solution)/shard_map/ppermute | solution.py:182
  791.9 36.7 %all-to-all-start.4 = ((bf16[16,2,128,1,256]{4,2,1,3,0:T(8,128)(2,1)}), bf16[16,2,128,1,256]{4,2,1,3,0:T(8,128)(2,1)}, u32[]{:S(2)}, u32[]{:S(2)}) async-start(bf16[16,2,128,1,256]{4,2,1,3,0:T(8,128)(2,1)} %broadcast_select_fusion), calls=%async_computation.6 | async-start | bytes 4194304 | tf_op jit(solution)/shard_map/all_to_all | solution.py:222
  798.7 87.9 %all-reduce.5.cloned.1.call-start = ((), (), s32[]{:S(2)}) async-start(), calls=%async_computation.11 | async-start | bytes 2097152 | tf_op jit(solution)/shard_map/psum | solution.py:199
  828.6 61.3 %copy-start.1 = (bf16[512,1280]{1,0:T(8,128)(2,1)S(1)}, bf16[512,1280]{1,0:T(8,128)(2,1)}, u32[]{:S(2)}) copy-start(bf16[512,1280]{1,0:T(8,128)(2,1)} %param.18) | copy-start | bytes 3932164
  (6 other events, 16.1 us)
Sparse Core Ops, SparseCore 0:
  57.2 76.2 reduce-scatter.2
  352.7 42.3 all-gather.1
  399.5 65.3 all-reduce.2
  523.9 168.1 reduce-scatter.4
  827.5 59.0 all-reduce.4
